TPU v7x, 32 devices: a whole 2x2x4 slice. The times are simulated.
32 devices in a mesh: section: 2 (over core), fsdp: 16 (over z, y, x).
Axes of the slice: x: 2, y: 2, z: 4, core: 2. Of those that a mesh axis runs over, the one named last changes fastest.
Arguments:
- tokens: bfloat16 [2, 2048, 2048], P(None, 'fsdp'), may hold values from -6 to 6
- norm_gains: float32 [2, 2048], P('section'), may hold values from 0.5 to 1.5
- router_cols: bfloat16 [2, 2048, 1], P('section'), may hold values from -0.125 to 0.125
- gate_weight: bfloat16 [2, 1, 1024, 2048], P('section', None, 'fsdp'), may hold values from -0.125 to 0.125
- up_weight: bfloat16 [2, 1, 1024, 2048], P('section', None, 'fsdp'), may hold values from -0.125 to 0.125
- down_weight: bfloat16 [2, 1, 1024, 2048], P('section', None, 'fsdp'), may hold values from -0.25 to 0.25
- expert_ids: int32 [2, 2, 2048, 8], P('section', None, 'fsdp'), may hold values from 0 to 63, all different within a row; in each aligned block of 128 rows (0 to 127, 128 to 255, ..., all dimensions but the last counted through in order) at most 32 rows name the same one
Outputs:
- layer_states: bfloat16 [2, 2, 2048, 2048], P('section', None, 'fsdp')
Inputs may be any that keep to these rules, and one draw needn't show every extreme that they name: `expert_ids`: within one layer and micro-batch, no expert is named by more than 32 of the 128 tokens of one fsdp index; a token names 8 different experts.
All inputs are finite; a program needn't handle non-finite values.
Results may differ from a plain program's by a relative error of at most 0.0013.
Values may be sent and summed in bfloat16 or wider, within the bound.
A program may use at most 128 MiB of HBM per device.

v0:
```python
import functools

import jax
import jax.numpy as jnp
from jax import lax
from jax.experimental import pallas as pl
from jax.experimental.pallas import tpu as pltpu
from jax.sharding import PartitionSpec as P

MESH = pl.DeviceIdType.MESH
BF16_ROWS = 16
PEERS = 4
RELEASE = 4
EPS = 1e-05


def silu(v):
    return v / (1.0 + jnp.exp(-v))


def across(lhs, rhs):
    return lax.dot_general(lhs, rhs, (((1,), (1,)), ((), ())), preferred_element_type=jnp.float32)


def plain(lhs, rhs):
    return jnp.dot(lhs, rhs, preferred_element_type=jnp.float32)


def kernel(
    n, most,
    tokens, gain, router, gate, up, down, ids,
    out,
    base, held, hnext, early, weights, picked, picked_in, gain_in, outc, outc_in, xbuf, xnext, pbuf, psend, mine,
    w_send, w_recv, x_send, x_recv, p_send, p_recv, o_send, o_recv, l_sem, go,
):
    sec = lax.axis_index("section")
    me = lax.axis_index("fsdp")
    far = n // 8
    micros, rows, width = tokens.shape
    hid = gate.shape[0]
    half = hid // 2
    slots = n // PEERS
    group_rows = PEERS * most

    bit_x = lax.rem(me, 2)
    bit_y = lax.rem(lax.div(me, 2), 2)
    bit_z = lax.rem(lax.div(me, 4), 2)
    by_x = 1 - 2 * bit_x
    by_y = 2 - 4 * bit_y
    by_z = 4 - 8 * bit_z
    by_t = by_x + sec * (by_y - by_x)
    peer = [me, me + by_t, me + by_z, me + by_t + by_z]
    cross = [me, me + by_y, me + by_z, me + by_y + by_z]
    beside = me + by_y + sec * (by_x - by_y)
    beyond = [lax.rem(me + 8 * d, n) for d in range(far)]
    other = 1 - sec

    barrier = pltpu.get_barrier_semaphore()
    met = [(sec, p) for p in peer[1:]] + [(sec, beside)] + [(sec, b) for b in beyond[1:]] + [(other, p) for p in cross]
    for device in met:
        pl.semaphore_signal(barrier, inc=1, device_id=device, device_id_type=MESH)

    own = (gate, up, down)
    chunks = [(a, h) for a in range(3) for h in range(2)]

    fetch = [pltpu.make_async_copy(tokens, base, l_sem.at[3])]
    fetch += [pltpu.make_async_copy(own[a], weights.at[a, pl.ds(0, hid)], l_sem.at[a]) for a in range(3)]
    for copy in fetch:
        copy.start()

    def weight_copy(slot, chunk, target, source_slot=None):
        a, h = chunks[chunk]
        span = pl.ds(h * half, half)
        if source_slot is None:
            src = own[a].at[span]
        else:
            src = weights.at[a, pl.ds(source_slot * hid + h * half, half)]
        return pltpu.make_async_remote_copy(
            src_ref=src,
            dst_ref=weights.at[a, pl.ds(slot * hid + h * half, half)],
            send_sem=w_send.at[slot, chunk],
            recv_sem=w_recv.at[slot, chunk],
            device_id=(sec, target),
            device_id_type=MESH,
        )

    def beside_copy(chunk):
        return weight_copy(1, chunk, beside)

    def first_copies(chunk):
        return [weight_copy(2 * (far - d), chunk, beyond[d]) for d in range(1, far)]

    def relay_copies(chunk):
        return [weight_copy(2 * r + 1, chunk, beside, 2 * r) for r in range(1, far)]

    def block(m, j):
        return pl.ds((m * PEERS + j) * most, most)

    def share_of(m):
        return pl.ds(m * most, most)

    def token_copy(m, j):
        return pltpu.make_async_remote_copy(
            src_ref=xbuf.at[block(m, 0)], dst_ref=xbuf.at[block(m, j)],
            send_sem=x_send.at[m, j], recv_sem=x_recv.at[m, j],
            device_id=(sec, peer[j]), device_id_type=MESH,
        )

    def token_relay(m):
        return pltpu.make_async_remote_copy(
            src_ref=xbuf.at[block(m, PEERS - 2)], dst_ref=xbuf.at[block(m, PEERS - 1)],
            send_sem=x_send.at[m, PEERS - 1], recv_sem=x_recv.at[m, PEERS - 1],
            device_id=(sec, peer[1]), device_id_type=MESH,
        )

    def onward_copy(m, j):
        return pltpu.make_async_remote_copy(
            src_ref=xnext.at[share_of(m)], dst_ref=xbuf.at[block(m, j)],
            send_sem=x_send.at[micros + m, j], recv_sem=x_recv.at[m, j],
            device_id=(other, cross[j]), device_id_type=MESH,
        )

    def partial_copy(m, j):
        return pltpu.make_async_remote_copy(
            src_ref=psend.at[block(m, j)], dst_ref=pbuf.at[block(m, j)],
            send_sem=p_send.at[m, j], recv_sem=p_recv.at[m, j],
            device_id=(sec, peer[j]), device_id_type=MESH,
        )

    def pass_copy(src, dst, k):
        return pltpu.make_async_remote_copy(
            src_ref=src, dst_ref=dst, send_sem=o_send.at[k], recv_sem=o_recv.at[k],
            device_id=(other, me), device_id_type=MESH,
        )

    pick_copy = pass_copy(picked, picked_in, 0)
    gain_copy = pass_copy(gain, gain_in, 1)
    held_copy = pass_copy(hnext, held, 2)
    outc_copy = pass_copy(outc, outc_in, 3)

    def norm(compact, scale):
        mean_square = jnp.mean(compact * compact, axis=-1, keepdims=True)
        return (compact * lax.rsqrt(mean_square + EPS) * scale).astype(jnp.bfloat16)

    def turned(picks):
        return jnp.transpose(picks.astype(jnp.float32))[0:most].astype(jnp.bfloat16)

    def merge(m, picks, compact, under):
        placed = plain(picks[m][:, 0:most], compact[m * most:(m + 1) * most, :])
        chosen = jnp.sum(picks[m].astype(jnp.float32), axis=1, keepdims=True) > 0.5
        return jnp.where(chosen, placed, under.astype(jnp.float32)).astype(jnp.bfloat16)

    pl.semaphore_wait(barrier, len(met))

    @pl.when(sec == 0)
    def _():
        for c in range(len(chunks)):
            for copy in first_copies(c):
                copy.start()

    @pl.when(sec == 1)
    def _():
        gain_copy.start()

    for c in range(len(chunks)):
        beside_copy(c).start()

    at_row = lax.broadcasted_iota(jnp.int32, (rows, rows), 0)
    at_col = lax.broadcasted_iota(jnp.int32, (rows, rows), 1)
    lower = jnp.where(at_row >= at_col, 1.0, 0.0).astype(jnp.bfloat16)
    for m in range(micros):
        named = jnp.sum(jnp.where(ids[m] == 0, 1.0, 0.0), axis=0, keepdims=True)
        spread = jnp.transpose(jnp.broadcast_to(named, (rows, rows)))
        rank = plain(lower, spread.astype(jnp.bfloat16))
        hit = (rank.astype(jnp.int32) - 1 == at_col) & (spread > 0.5)
        picked[m] = jnp.where(hit, 1.0, 0.0).astype(jnp.bfloat16)
    pick_copy.start()
    for copy in fetch:
        copy.wait()

    @pl.when(sec == 0)
    def _():
        for m in range(micros):
            compact = plain(turned(picked[m]), base[m])
            held[share_of(m), :] = compact.astype(jnp.bfloat16)
            xbuf[block(m, 0), :] = norm(compact, gain[...])
            for j in range(1, PEERS - 1):
                token_copy(m, j).start()
        pick_copy.wait_recv()
        gain_copy.wait_recv()
        for m in range(micros):
            early[share_of(m), :] = plain(turned(picked_in[m]), base[m])

    @pl.when(sec == 1)
    def _():
        pl.semaphore_wait(go, 1)
        for c in range(len(chunks)):
            for copy in first_copies(c):
                copy.start()
        pick_copy.wait_recv()

    for c in range(len(chunks)):
        for come, onward in zip(first_copies(c), relay_copies(c)):
            come.wait_recv()
            onward.start()
            come.wait_send()
        if c == 1:
            @pl.when(sec == 0)
            def _():
                for m in range(micros):
                    token_copy(m, PEERS - 2).wait_recv()
                    token_relay(m).start()
        if c == RELEASE:
            @pl.when(sec == 0)
            def _():
                pl.semaphore_signal(go, inc=1, device_id=(other, me), device_id_type=MESH)

    def wait_weights(some):
        for c in some:
            beside_copy(c).wait_recv()
            for copy in relay_copies(c):
                copy.wait_recv()

    wait_weights(range(4))

    @pl.when(sec == 0)
    def _():
        for m in range(micros):
            token_copy(m, 1).wait_recv()
            token_relay(m).wait_recv()

    for m in range(micros):
        @pl.when(sec == 1)
        def _():
            for j in range(PEERS):
                onward_copy(m, j).wait_recv()

        x = xbuf[pl.ds(m * group_rows, group_rows), :]
        activated = (silu(across(x, weights[0])) * across(x, weights[1])).astype(jnp.bfloat16)
        if m == 0:
            wait_weights(range(4, len(chunks)))
        partial = plain(activated, weights[2])
        mine[share_of(m), :] = partial[0:most]
        psend[pl.ds(m * group_rows, group_rows), :] = partial.astype(jnp.bfloat16)
        for j in range(PEERS - 1, 0, -1):
            partial_copy(m, j).start()

    @pl.when(sec == 1)
    def _():
        held_copy.wait_recv()
        outc_copy.wait_recv()
        for m in range(micros):
            base[m] = merge(m, picked_in, outc_in, base[m])

    for m in range(micros):
        span = share_of(m)
        score = jnp.sum(xbuf[block(m, 0), :].astype(jnp.float32) * router[...].astype(jnp.float32), axis=1, keepdims=True)
        share = 1.0 / (1.0 + jnp.exp(-score))
        update = mine[span, :]
        for j in range(1, PEERS):
            partial_copy(m, j).wait_recv()
            update = update + pbuf[block(m, j), :].astype(jnp.float32)
        outc[span, :] = (held[span, :].astype(jnp.float32) + share * update).astype(jnp.bfloat16)

        @pl.when(sec == 0)
        def _():
            again = plain(turned(picked_in[m]), picked[m][:, 0:most])
            changed = jnp.sum(again, axis=1, keepdims=True) > 0.5
            following = jnp.where(changed, plain(again.astype(jnp.bfloat16), outc[span, :]), early[span, :])
            xnext[span, :] = norm(following, gain_in[...])
            hnext[span, :] = following.astype(jnp.bfloat16)
            for j in range(PEERS - 1, -1, -1):
                onward_copy(m, j).start()

        @pl.when(sec == 1)
        def _():
            out[m] = merge(m, picked, outc, base[m])

    @pl.when(sec == 0)
    def _():
        held_copy.start()
        outc_copy.start()
        for m in range(micros):
            out[m] = merge(m, picked, outc, base[m])

    for c in range(len(chunks)):
        beside_copy(c).wait_send()
        for copy in relay_copies(c):
            copy.wait_send()
    pick_copy.wait_send()
    for m in range(micros):
        for j in range(1, PEERS):
            partial_copy(m, j).wait_send()

    @pl.when(sec == 0)
    def _():
        held_copy.wait_send()
        outc_copy.wait_send()
        for m in range(micros):
            for j in range(1, PEERS - 1):
                token_copy(m, j).wait_send()
            token_relay(m).wait_send()
            for j in range(PEERS):
                onward_copy(m, j).wait_send()

    @pl.when(sec == 1)
    def _():
        gain_copy.wait_send()


def grouped(n, tokens, norm_gains, router_cols, gate_weight, up_weight, down_weight, expert_ids):
    micros, rows, width = tokens.shape
    hid = gate_weight.shape[2]
    most = rows // 4
    slots = n // PEERS
    own_rows = micros * most
    all_rows = PEERS * own_rows
    dma = pltpu.SemaphoreType.DMA
    vmem = pl.BlockSpec(memory_space=pltpu.VMEM)
    whole = pl.BlockSpec(memory_space=pltpu.HBM)
    half = lambda *shape: pltpu.VMEM(shape, jnp.bfloat16)
    full = lambda *shape: pltpu.VMEM(shape, jnp.float32)
    result = pl.pallas_call(
        functools.partial(kernel, n, most),
        out_shape=jax.ShapeDtypeStruct((micros, rows, width), jnp.bfloat16),
        in_specs=[whole, vmem, vmem, whole, whole, whole, vmem],
        out_specs=vmem,
        scratch_shapes=[
            half(micros, rows, width),
            half(own_rows, width),
            half(own_rows, width),
            full(own_rows, width),
            half(3, slots * hid, width),
            half(micros, rows, rows),
            half(micros, rows, rows),
            full(1, width),
            half(own_rows, width),
            half(own_rows, width),
            half(all_rows, width),
            half(own_rows, width),
            half(all_rows, width),
            half(all_rows, width),
            full(own_rows, width),
            dma((slots, 6)), dma((slots, 6)),
            dma((2 * micros, PEERS)), dma((micros, PEERS)), dma((micros, PEERS)), dma((micros, PEERS)),
            dma((4,)), dma((4,)), dma((4,)),
            pltpu.SemaphoreType.REGULAR,
        ],
        compiler_params=pltpu.CompilerParams(
            collective_id=0, has_side_effects=True, vmem_limit_bytes=67_000_000
        ),
    )(
        tokens, norm_gains, router_cols.reshape(1, width),
        gate_weight[0, 0], up_weight[0, 0], down_weight[0, 0], jnp.swapaxes(expert_ids[0], 1, 2),
    )
    return result[None]


def gathered(tokens, norm_gains, router_cols, gate_weight, up_weight, down_weight, expert_ids):
    section = lax.axis_index("section")
    micros, rows, width = tokens.shape
    stacked = jnp.stack((gate_weight[0, 0], up_weight[0, 0], down_weight[0, 0]))
    panels = lax.all_gather(stacked, "fsdp", axis=1, tiled=True)
    gate, up, down = panels[0], panels[1], panels[2]

    def layer(hidden, routed):
        widened = hidden.astype(jnp.float32)
        mean_square = jnp.mean(widened * widened, axis=-1, keepdims=True)
        normed = (widened * lax.rsqrt(mean_square + EPS) * norm_gains[0]).astype(jnp.bfloat16)
        score = jax.nn.sigmoid(plain(normed, router_cols[0]))[:, 0]
        weight = jnp.where(jnp.any(routed == 0, axis=-1), score, jnp.zeros_like(score))
        activated = (jax.nn.silu(across(normed, gate)) * across(normed, up)).astype(jnp.bfloat16)
        return (widened + weight[:, None] * plain(activated, down)).astype(jnp.bfloat16)

    first = [layer(tokens[m], expert_ids[0, m]) for m in range(micros)]
    coming = [lax.ppermute(f, "section", [(0, 1)]) for f in first]
    second = [layer(coming[m], expert_ids[0, m]) for m in range(micros)]
    return jnp.where(section == 0, jnp.stack(first), jnp.stack(second))[None]


def solution(mesh):
    n = mesh.shape["fsdp"]

    def local(*args):
        hid = args[3].shape[2]
        if n % 8 == 0 and hid % (2 * BF16_ROWS) == 0:
            return grouped(n, *args)
        return gathered(*args)

    in_specs = (
        P(None, "fsdp", None),
        P("section", None),
        P("section", None, None),
        P("section", None, "fsdp", None),
        P("section", None, "fsdp", None),
        P("section", None, "fsdp", None),
        P("section", None, "fsdp", None),
    )
    out_specs = P("section", None, "fsdp", None)
    return jax.shard_map(local, mesh=mesh, in_specs=in_specs, out_specs=out_specs, check_vma=False)
```

profile of v0, /device:TPU:1, one launch (start us, length us, event | category | flops | bytes accessed | tf_op | source)
XLA Modules:
  0.0 58.9 jit_solution(11718580066051982400)
XLA Ops:
  0.0 56.6 %shard_map.73 = bf16[2,128,2048]{2,1,0:T(8,128)(2,1)} custom-call(bf16[2,128,2048]{2,1,0:T(8,128)(2,1)} %tokens.1, f32[1,2048]{1,0:T(1,128)} %gain.1, bf16[1,2048]{1,0:T(2,128)(2,1)} %bitcast.12, bf16[64,2048]{1,0:T(8,128)(2,1)} %bitcast.9, bf16[64,2048]{1,0:T(8,128)(2,1)} %bitcast.10, bf16[64,2048]{1,0:T(8,128)(2,1)} %bitcast.11, s32[2,8,128]{2,1,0:T(8,128)} %bitcast.13), custom_call_target="tpu_custom_call" | custom-call | tf_op jit(solution)/shard_map/pallas_call | solution.py:323
  56.6 2.3 %copy.9 = bf16[1,2,128,2048]{3,2,1,0:T(8,128)(2,1)} copy(bf16[1,2,128,2048]{3,2,1,0:T(8,128)(2,1)} %bitcast.8) | data formatting | bytes 2097152
where the time goes:
time: 59.1 us; the launch traced here: 58.9 us
  Pallas kernels  56.6 us (96%)
  local copies, waits for them, and re-layouts  2.3 us (4%)
    pallas_call x1, Pallas kernels, grouped(): pl.pallas_call(functools.partial(kernel, n, most), out_shape=jax.ShapeDty...  56.6 us
    unnamed x1, local copies, waits for them, and re-layouts  2.3 us

commit v1 on v0

--- a/solution.py
+++ b/solution.py
@@ -10,7 +10,8 @@
 MESH = pl.DeviceIdType.MESH
 BF16_ROWS = 16
 PEERS = 4
-RELEASE = 4
+AHEAD = 4
+FIRST = 0
 EPS = 1e-05
 
 
@@ -30,33 +31,30 @@
     n, most,
     tokens, gain, router, gate, up, down, ids,
     out,
-    base, held, hnext, early, weights, picked, picked_in, gain_in, outc, outc_in, xbuf, xnext, pbuf, psend, mine,
+    base, held, hnext, early, weights, picked, picked_in, gain_in, outc, outc_in, xbuf, xnext, pbuf, psend, mine, across_part,
     w_send, w_recv, x_send, x_recv, p_send, p_recv, o_send, o_recv, l_sem, go,
 ):
     sec = lax.axis_index("section")
     me = lax.axis_index("fsdp")
-    far = n // 8
     micros, rows, width = tokens.shape
     hid = gate.shape[0]
     half = hid // 2
-    slots = n // PEERS
     group_rows = PEERS * most
-
-    bit_x = lax.rem(me, 2)
-    bit_y = lax.rem(lax.div(me, 2), 2)
-    bit_z = lax.rem(lax.div(me, 4), 2)
-    by_x = 1 - 2 * bit_x
-    by_y = 2 - 4 * bit_y
-    by_z = 4 - 8 * bit_z
-    by_t = by_x + sec * (by_y - by_x)
-    peer = [me, me + by_t, me + by_z, me + by_t + by_z]
+    other = 1 - sec
+
+    by_x = 1 - 2 * lax.rem(me, 2)
+    by_y = 2 - 4 * lax.rem(lax.div(me, 2), 2)
+    by_z = 4 - 8 * lax.rem(lax.div(me, 4), 2)
+    by_far = 8 - 16 * lax.rem(lax.div(me, 8), 2)
+    near = [me, me + by_z, me + by_far, me + by_z + by_far]
     cross = [me, me + by_y, me + by_z, me + by_y + by_z]
-    beside = me + by_y + sec * (by_x - by_y)
-    beyond = [lax.rem(me + 8 * d, n) for d in range(far)]
-    other = 1 - sec
+    peer = [a + sec * (b - a) for a, b in zip(near, cross)]
+    at_x = me + by_x
+    at_y = me + by_y
+    far = me + by_far
 
     barrier = pltpu.get_barrier_semaphore()
-    met = [(sec, p) for p in peer[1:]] + [(sec, beside)] + [(sec, b) for b in beyond[1:]] + [(other, p) for p in cross]
+    met = [(sec, p) for p in [at_x, at_y, me + by_z, far, me + by_z + by_far, me + by_y + by_z]] + [(other, p) for p in cross]
     for device in met:
         pl.semaphore_signal(barrier, inc=1, device_id=device, device_id_type=MESH)
 
@@ -84,14 +82,22 @@
             device_id_type=MESH,
         )
 
-    def beside_copy(chunk):
-        return weight_copy(1, chunk, beside)
-
-    def first_copies(chunk):
-        return [weight_copy(2 * (far - d), chunk, beyond[d]) for d in range(1, far)]
-
-    def relay_copies(chunk):
-        return [weight_copy(2 * r + 1, chunk, beside, 2 * r) for r in range(1, far)]
+    def x_copy(chunk):
+        return weight_copy(1, chunk, at_x)
+
+    def y_copy(chunk):
+        return weight_copy(2, chunk, at_y)
+
+    def far_copy(chunk):
+        return weight_copy(2, chunk, far)
+
+    def turn_copy(chunk):
+        if chunk % 2 == 0:
+            return weight_copy(3, chunk, at_x, 2)
+        return weight_copy(3, chunk, at_y, 1)
+
+    def far_turn_copy(chunk):
+        return weight_copy(3, chunk, at_x, 2)
 
     def block(m, j):
         return pl.ds((m * PEERS + j) * most, most)
@@ -125,6 +131,13 @@
             src_ref=psend.at[block(m, j)], dst_ref=pbuf.at[block(m, j)],
             send_sem=p_send.at[m, j], recv_sem=p_recv.at[m, j],
             device_id=(sec, peer[j]), device_id_type=MESH,
+        )
+
+    def early_copy(m):
+        return pltpu.make_async_remote_copy(
+            src_ref=psend.at[block(m, PEERS - 1)], dst_ref=pbuf.at[block(m, PEERS - 1)],
+            send_sem=p_send.at[m, PEERS - 1], recv_sem=p_recv.at[m, PEERS - 1],
+            device_id=(sec, peer[1]), device_id_type=MESH,
         )
 
     def pass_copy(src, dst, k):
@@ -150,33 +163,18 @@
         chosen = jnp.sum(picks[m].astype(jnp.float32), axis=1, keepdims=True) > 0.5
         return jnp.where(chosen, placed, under.astype(jnp.float32)).astype(jnp.bfloat16)
 
-    pl.semaphore_wait(barrier, len(met))
-
-    @pl.when(sec == 0)
-    def _():
-        for c in range(len(chunks)):
-            for copy in first_copies(c):
-                copy.start()
-
-    @pl.when(sec == 1)
-    def _():
-        gain_copy.start()
-
-    for c in range(len(chunks)):
-        beside_copy(c).start()
-
-    at_row = lax.broadcasted_iota(jnp.int32, (rows, rows), 0)
-    at_col = lax.broadcasted_iota(jnp.int32, (rows, rows), 1)
-    lower = jnp.where(at_row >= at_col, 1.0, 0.0).astype(jnp.bfloat16)
-    for m in range(micros):
-        named = jnp.sum(jnp.where(ids[m] == 0, 1.0, 0.0), axis=0, keepdims=True)
-        spread = jnp.transpose(jnp.broadcast_to(named, (rows, rows)))
-        rank = plain(lower, spread.astype(jnp.bfloat16))
-        hit = (rank.astype(jnp.int32) - 1 == at_col) & (spread > 0.5)
-        picked[m] = jnp.where(hit, 1.0, 0.0).astype(jnp.bfloat16)
-    pick_copy.start()
-    for copy in fetch:
-        copy.wait()
+    with jax.named_scope("pick"):
+        at_row = lax.broadcasted_iota(jnp.int32, (rows, rows), 0)
+        at_col = lax.broadcasted_iota(jnp.int32, (rows, rows), 1)
+        lower = jnp.where(at_row >= at_col, 1.0, 0.0).astype(jnp.bfloat16)
+        for m in range(micros):
+            named = jnp.sum(jnp.where(ids[m] == 0, 1.0, 0.0), axis=0, keepdims=True)
+            spread = jnp.transpose(jnp.broadcast_to(named, (rows, rows)))
+            rank = plain(lower, spread.astype(jnp.bfloat16))
+            hit = (rank.astype(jnp.int32) - 1 == at_col) & (spread > 0.5)
+            picked[m] = jnp.where(hit, 1.0, 0.0).astype(jnp.bfloat16)
+        for copy in fetch:
+            copy.wait()
 
     @pl.when(sec == 0)
     def _():
@@ -184,66 +182,134 @@
             compact = plain(turned(picked[m]), base[m])
             held[share_of(m), :] = compact.astype(jnp.bfloat16)
             xbuf[block(m, 0), :] = norm(compact, gain[...])
-            for j in range(1, PEERS - 1):
+
+    with jax.named_scope("bar"):
+        pl.semaphore_wait(barrier, len(met))
+
+    @pl.when(sec == 0)
+    def _():
+        for m in range(micros):
+            for j in range(PEERS - 2, 0, -1):
                 token_copy(m, j).start()
+        for c in range(len(chunks)):
+            x_copy(c).start()
+            y_copy(c).start()
+        pick_copy.start()
         pick_copy.wait_recv()
         gain_copy.wait_recv()
         for m in range(micros):
+            token_copy(m, PEERS - 2).wait_send()
+        pl.semaphore_signal(go.at[0], inc=1, device_id=(other, me), device_id_type=MESH)
+        for m in range(micros):
             early[share_of(m), :] = plain(turned(picked_in[m]), base[m])
 
+        with jax.named_scope("xrelay"):
+            for m in range(micros):
+                token_copy(m, PEERS - 2).wait_recv()
+                token_relay(m).start()
+        for c in range(len(chunks)):
+            with jax.named_scope("wrelay"):
+                (y_copy if c % 2 == 0 else x_copy)(c).wait_recv()
+            turn_copy(c).start()
+
     @pl.when(sec == 1)
     def _():
-        pl.semaphore_wait(go, 1)
-        for c in range(len(chunks)):
-            for copy in first_copies(c):
-                copy.start()
+        for c in range(FIRST):
+            far_copy(c).start()
+        gain_copy.start()
+        pick_copy.start()
         pick_copy.wait_recv()
-
-    for c in range(len(chunks)):
-        for come, onward in zip(first_copies(c), relay_copies(c)):
-            come.wait_recv()
-            onward.start()
-            come.wait_send()
-        if c == 1:
+        with jax.named_scope("go0"):
+            pl.semaphore_wait(go.at[0], 1)
+        for c in range(FIRST, AHEAD):
+            far_copy(c).start()
+        with jax.named_scope("go1"):
+            pl.semaphore_wait(go.at[1], 1)
+        for c in range(AHEAD):
+            x_copy(c).start()
+            with jax.named_scope("frelay"):
+                far_copy(c).wait_recv()
+            far_turn_copy(c).start()
+        for c in range(AHEAD, len(chunks)):
+            x_copy(c).start()
+        with jax.named_scope("go2"):
+            pl.semaphore_wait(go.at[2], 1)
+        for c in range(AHEAD, len(chunks)):
+            far_copy(c).start()
+        for c in range(AHEAD, len(chunks)):
+            with jax.named_scope("frelay"):
+                far_copy(c).wait_recv()
+            far_turn_copy(c).start()
+
+    def wait_weights(some):
+        for c in some:
             @pl.when(sec == 0)
             def _():
-                for m in range(micros):
-                    token_copy(m, PEERS - 2).wait_recv()
-                    token_relay(m).start()
-        if c == RELEASE:
+                (x_copy if c % 2 == 0 else y_copy)(c).wait_recv()
+                turn_copy(c).wait_recv()
+
+            @pl.when(sec == 1)
+            def _():
+                x_copy(c).wait_recv()
+                far_turn_copy(c).wait_recv()
+
+    with jax.named_scope("ww"):
+        wait_weights(range(4))
+
+    @pl.when(sec == 0)
+    def _():
+        with jax.named_scope("wtok"):
+            for m in range(micros):
+                token_copy(m, 1).wait_recv()
+                token_relay(m).wait_recv()
+
+    for m in range(micros):
+        @pl.when(sec == 1)
+        def _():
+            with jax.named_scope("won"):
+                for j in range(PEERS):
+                    onward_copy(m, j).wait_recv()
+
+        with jax.named_scope("gu"):
+            x = xbuf[pl.ds(m * group_rows, group_rows), :]
+            activated = (silu(across(x, weights[0])) * across(x, weights[1])).astype(jnp.bfloat16)
+        if m == 0:
+            with jax.named_scope("ww2"):
+                wait_weights(range(4, len(chunks)))
+
             @pl.when(sec == 0)
             def _():
-                pl.semaphore_signal(go, inc=1, device_id=(other, me), device_id_type=MESH)
-
-    def wait_weights(some):
-        for c in some:
-            beside_copy(c).wait_recv()
-            for copy in relay_copies(c):
-                copy.wait_recv()
-
-    wait_weights(range(4))
-
-    @pl.when(sec == 0)
-    def _():
-        for m in range(micros):
-            token_copy(m, 1).wait_recv()
-            token_relay(m).wait_recv()
-
-    for m in range(micros):
+                pl.semaphore_signal(go.at[1], inc=1, device_id=(other, me), device_id_type=MESH)
+
+        with jax.named_scope("down"):
+            partial = plain(activated, weights[2])
+            mine[share_of(m), :] = partial[0:most]
+            psend[pl.ds(m * group_rows, group_rows), :] = partial.astype(jnp.bfloat16)
+        @pl.when(sec == 0)
+        def _():
+            across_part[share_of(m), :] = partial[2 * most:3 * most]
+            early_copy(m).start()
+            if m == micros - 1:
+                for k in range(micros):
+                    partial_copy(k, 1).start()
+
         @pl.when(sec == 1)
         def _():
-            for j in range(PEERS):
-                onward_copy(m, j).wait_recv()
-
-        x = xbuf[pl.ds(m * group_rows, group_rows), :]
-        activated = (silu(across(x, weights[0])) * across(x, weights[1])).astype(jnp.bfloat16)
-        if m == 0:
-            wait_weights(range(4, len(chunks)))
-        partial = plain(activated, weights[2])
-        mine[share_of(m), :] = partial[0:most]
-        psend[pl.ds(m * group_rows, group_rows), :] = partial.astype(jnp.bfloat16)
-        for j in range(PEERS - 1, 0, -1):
-            partial_copy(m, j).start()
+            for j in range(PEERS - 1, 0, -1):
+                partial_copy(m, j).start()
+
+    @pl.when(sec == 0)
+    def _():
+        for m in range(micros):
+            with jax.named_scope("wearly"):
+                early_copy(m).wait_recv()
+            joined = across_part[share_of(m), :] + pbuf[block(m, PEERS - 1), :].astype(jnp.float32)
+            psend[block(m, 2), :] = joined.astype(jnp.bfloat16)
+            partial_copy(m, 2).start()
+        for m in range(micros):
+            with jax.named_scope("wsent"):
+                partial_copy(m, 2).wait_send()
+        pl.semaphore_signal(go.at[2], inc=1, device_id=(other, me), device_id_type=MESH)
 
     @pl.when(sec == 1)
     def _():
@@ -254,21 +320,28 @@
 
     for m in range(micros):
         span = share_of(m)
-        score = jnp.sum(xbuf[block(m, 0), :].astype(jnp.float32) * router[...].astype(jnp.float32), axis=1, keepdims=True)
-        share = 1.0 / (1.0 + jnp.exp(-score))
-        update = mine[span, :]
-        for j in range(1, PEERS):
-            partial_copy(m, j).wait_recv()
-            update = update + pbuf[block(m, j), :].astype(jnp.float32)
+        with jax.named_scope("wpart"):
+            score = jnp.sum(xbuf[block(m, 0), :].astype(jnp.float32) * router[...].astype(jnp.float32), axis=1, keepdims=True)
+            share = 1.0 / (1.0 + jnp.exp(-score))
+            for j in range(1, PEERS - 1):
+                partial_copy(m, j).wait_recv()
+            last = partial_copy(m, PEERS - 1)
+            pl.when(sec == 1)(last.wait_recv)
+            update = mine[span, :]
+            for j in range(1, PEERS - 1):
+                update = update + pbuf[block(m, j), :].astype(jnp.float32)
+            over = pbuf[block(m, PEERS - 1), :].astype(jnp.float32)
+            update = update + jnp.where(sec == 1, over, 0.0)
         outc[span, :] = (held[span, :].astype(jnp.float32) + share * update).astype(jnp.bfloat16)
 
         @pl.when(sec == 0)
         def _():
-            again = plain(turned(picked_in[m]), picked[m][:, 0:most])
-            changed = jnp.sum(again, axis=1, keepdims=True) > 0.5
-            following = jnp.where(changed, plain(again.astype(jnp.bfloat16), outc[span, :]), early[span, :])
-            xnext[span, :] = norm(following, gain_in[...])
-            hnext[span, :] = following.astype(jnp.bfloat16)
+            with jax.named_scope("next"):
+                again = plain(turned(picked_in[m]), picked[m][:, 0:most])
+                changed = jnp.sum(again, axis=1, keepdims=True) > 0.5
+                following = jnp.where(changed, plain(again.astype(jnp.bfloat16), outc[span, :]), early[span, :])
+                xnext[span, :] = norm(following, gain_in[...])
+                hnext[span, :] = following.astype(jnp.bfloat16)
             for j in range(PEERS - 1, -1, -1):
                 onward_copy(m, j).start()
 
@@ -284,21 +357,36 @@
             out[m] = merge(m, picked, outc, base[m])
 
     for c in range(len(chunks)):
-        beside_copy(c).wait_send()
-        for copy in relay_copies(c):
-            copy.wait_send()
+        x_copy(c).wait_send()
+
+        @pl.when(sec == 0)
+        def _():
+            y_copy(c).wait_send()
+            turn_copy(c).wait_send()
+
+        @pl.when(sec == 1)
+        def _():
+            far_copy(c).wait_send()
+            far_turn_copy(c).wait_send()
     pick_copy.wait_send()
     for m in range(micros):
-        for j in range(1, PEERS):
-            partial_copy(m, j).wait_send()
+        partial_copy(m, 1).wait_send()
+
+        @pl.when(sec == 0)
+        def _():
+            early_copy(m).wait_send()
+
+        @pl.when(sec == 1)
+        def _():
+            partial_copy(m, 2).wait_send()
+            partial_copy(m, PEERS - 1).wait_send()
 
     @pl.when(sec == 0)
     def _():
         held_copy.wait_send()
         outc_copy.wait_send()
         for m in range(micros):
-            for j in range(1, PEERS - 1):
-                token_copy(m, j).wait_send()
+            token_copy(m, 1).wait_send()
             token_relay(m).wait_send()
             for j in range(PEERS):
                 onward_copy(m, j).wait_send()
@@ -341,10 +429,11 @@
             half(all_rows, width),
             half(all_rows, width),
             full(own_rows, width),
+            full(own_rows, width),
             dma((slots, 6)), dma((slots, 6)),
             dma((2 * micros, PEERS)), dma((micros, PEERS)), dma((micros, PEERS)), dma((micros, PEERS)),
             dma((4,)), dma((4,)), dma((4,)),
-            pltpu.SemaphoreType.REGULAR,
+            pltpu.SemaphoreType.REGULAR((3,)),
         ],
         compiler_params=pltpu.CompilerParams(
             collective_id=0, has_side_effects=True, vmem_limit_bytes=67_000_000
@@ -383,7 +472,7 @@
 
     def local(*args):
         hid = args[3].shape[2]
-        if n % 8 == 0 and hid % (2 * BF16_ROWS) == 0:
+        if n == PEERS * PEERS and hid % (2 * BF16_ROWS) == 0:
             return grouped(n, *args)
         return gathered(*args)
 

time: 59.1 us -> 56.8 us (0.961)
  Pallas kernels: 56.6 us -> 54.2 us
    pallas_call x1, Pallas kernels: 56.6 us -> 54.2 us  [grouped(): pl.pallas_call(functools.partial(kernel, n, most), out_shape=jax.ShapeDty...]
where the time goes in v1:
time: 56.8 us; the launch traced here: 56.5 us
  Pallas kernels  54.2 us (95%)
  local copies, waits for them, and re-layouts  2.3 us (4%)
    pallas_call x1, Pallas kernels, grouped(): pl.pallas_call(functools.partial(kernel, n, most), out_shape=jax.ShapeDty...  54.2 us
    unnamed x1, local copies, waits for them, and re-layouts  2.3 us

profile of v1, /device:TPU:1, one launch (start us, length us, event | category | flops | bytes accessed | tf_op | source)
XLA Modules:
  0.0 56.5 jit_solution(11750760352096713691)
XLA Ops:
  0.0 54.2 %shard_map.73 = bf16[2,128,2048]{2,1,0:T(8,128)(2,1)} custom-call(bf16[2,128,2048]{2,1,0:T(8,128)(2,1)} %tokens.1, f32[1,2048]{1,0:T(1,128)} %gain.1, bf16[1,2048]{1,0:T(2,128)(2,1)} %bitcast.12, bf16[64,2048]{1,0:T(8,128)(2,1)} %bitcast.9, bf16[64,2048]{1,0:T(8,128)(2,1)} %bitcast.10, bf16[64,2048]{1,0:T(8,128)(2,1)} %bitcast.11, s32[2,8,128]{2,1,0:T(8,128)} %bitcast.13), custom_call_target="tpu_custom_call" | custom-call | tf_op jit(solution)/shard_map/pallas_call | solution.py:411
  54.2 2.3 %copy.9 = bf16[1,2,128,2048]{3,2,1,0:T(8,128)(2,1)} copy(bf16[1,2,128,2048]{3,2,1,0:T(8,128)(2,1)} %bitcast.8) | data formatting | bytes 2097152

commit v2 on v1

--- a/solution.py
+++ b/solution.py
@@ -10,7 +10,8 @@
 MESH = pl.DeviceIdType.MESH
 BF16_ROWS = 16
 PEERS = 4
-AHEAD = 4
+AHEAD = 10
+CUTS = 2
 FIRST = 0
 EPS = 1e-05
 
@@ -31,14 +32,16 @@
     n, most,
     tokens, gain, router, gate, up, down, ids,
     out,
-    base, held, hnext, early, weights, picked, picked_in, gain_in, outc, outc_in, xbuf, xnext, pbuf, psend, mine, across_part,
+    base, held, hnext, early, weights, picked, picked_in, gain_in, outc, outc_in, xbuf, xnext, pbuf, psend, mine, across_part, rest,
     w_send, w_recv, x_send, x_recv, p_send, p_recv, o_send, o_recv, l_sem, go,
 ):
     sec = lax.axis_index("section")
     me = lax.axis_index("fsdp")
     micros, rows, width = tokens.shape
     hid = gate.shape[0]
-    half = hid // 2
+    parts = hid // BF16_ROWS
+    half = hid // parts
+    pieces = most // BF16_ROWS
     group_rows = PEERS * most
     other = 1 - sec
 
@@ -52,6 +55,8 @@
     at_x = me + by_x
     at_y = me + by_y
     far = me + by_far
+    inner = lax.rem(lax.div(me, 4) + lax.div(me, 8), 2) == 1
+    outer = jnp.logical_not(inner)
 
     barrier = pltpu.get_barrier_semaphore()
     met = [(sec, p) for p in [at_x, at_y, me + by_z, far, me + by_z + by_far, me + by_y + by_z]] + [(other, p) for p in cross]
@@ -59,14 +64,14 @@
         pl.semaphore_signal(barrier, inc=1, device_id=device, device_id_type=MESH)
 
     own = (gate, up, down)
-    chunks = [(a, h) for a in range(3) for h in range(2)]
+    chunks = [(a, h) for a in range(3) for h in range(parts)]
 
     fetch = [pltpu.make_async_copy(tokens, base, l_sem.at[3])]
     fetch += [pltpu.make_async_copy(own[a], weights.at[a, pl.ds(0, hid)], l_sem.at[a]) for a in range(3)]
     for copy in fetch:
         copy.start()
 
-    def weight_copy(slot, chunk, target, source_slot=None):
+    def weight_copy(slot, chunk, target, send, recv, source_slot=None):
         a, h = chunks[chunk]
         span = pl.ds(h * half, half)
         if source_slot is None:
@@ -76,28 +81,53 @@
         return pltpu.make_async_remote_copy(
             src_ref=src,
             dst_ref=weights.at[a, pl.ds(slot * hid + h * half, half)],
-            send_sem=w_send.at[slot, chunk],
-            recv_sem=w_recv.at[slot, chunk],
+            send_sem=w_send.at[send],
+            recv_sem=w_recv.at[recv],
             device_id=(sec, target),
             device_id_type=MESH,
         )
 
-    def x_copy(chunk):
-        return weight_copy(1, chunk, at_x)
-
-    def y_copy(chunk):
-        return weight_copy(2, chunk, at_y)
+    count = len(chunks)
+    early_chunks = 2 * parts
+
+    def group(k, chunk):
+        return count + 2 * k + (1 if chunk >= early_chunks else 0)
+
+    def x_copy(chunk, single=False):
+        return weight_copy(1, chunk, at_x, 0, chunk if single else group(0, chunk))
+
+    def y_copy(chunk, single=False):
+        return weight_copy(2, chunk, at_y, 1, chunk if single else group(1, chunk))
+
+    def own_copies(chunk):
+        return [x_copy(chunk, chunk % 2 == 1), y_copy(chunk, chunk % 2 == 0)]
 
     def far_copy(chunk):
-        return weight_copy(2, chunk, far)
+        return weight_copy(2, chunk, far, 1, chunk)
 
     def turn_copy(chunk):
         if chunk % 2 == 0:
-            return weight_copy(3, chunk, at_x, 2)
-        return weight_copy(3, chunk, at_y, 1)
+            return weight_copy(3, chunk, at_x, 2, group(2, chunk), 2)
+        return weight_copy(3, chunk, at_y, 3, group(2, chunk), 1)
 
     def far_turn_copy(chunk):
-        return weight_copy(3, chunk, at_x, 2)
+        return weight_copy(3, chunk, at_x, 2, group(2, chunk), 2)
+
+    def sent(sems, k, ref, some):
+        bulk = pltpu.make_async_remote_copy(
+            src_ref=ref.at[pl.ds(0, some)], dst_ref=ref.at[pl.ds(0, some)],
+            send_sem=sems.at[k], recv_sem=sems.at[k],
+            device_id=(other, me), device_id_type=MESH,
+        )
+        bulk.wait_send()
+
+    def got(sems, k, ref, some):
+        bulk = pltpu.make_async_remote_copy(
+            src_ref=ref.at[pl.ds(0, some)], dst_ref=ref.at[pl.ds(0, some)],
+            send_sem=sems.at[k], recv_sem=sems.at[k],
+            device_id=(other, me), device_id_type=MESH,
+        )
+        bulk.wait_recv()
 
     def block(m, j):
         return pl.ds((m * PEERS + j) * most, most)
@@ -108,37 +138,50 @@
     def token_copy(m, j):
         return pltpu.make_async_remote_copy(
             src_ref=xbuf.at[block(m, 0)], dst_ref=xbuf.at[block(m, j)],
-            send_sem=x_send.at[m, j], recv_sem=x_recv.at[m, j],
+            send_sem=x_send.at[j - 1], recv_sem=x_recv.at[m if j == 2 else micros],
             device_id=(sec, peer[j]), device_id_type=MESH,
         )
 
     def token_relay(m):
         return pltpu.make_async_remote_copy(
             src_ref=xbuf.at[block(m, PEERS - 2)], dst_ref=xbuf.at[block(m, PEERS - 1)],
-            send_sem=x_send.at[m, PEERS - 1], recv_sem=x_recv.at[m, PEERS - 1],
+            send_sem=x_send.at[0], recv_sem=x_recv.at[micros],
             device_id=(sec, peer[1]), device_id_type=MESH,
         )
 
     def onward_copy(m, j):
         return pltpu.make_async_remote_copy(
             src_ref=xnext.at[share_of(m)], dst_ref=xbuf.at[block(m, j)],
-            send_sem=x_send.at[micros + m, j], recv_sem=x_recv.at[m, j],
+            send_sem=x_send.at[2], recv_sem=x_recv.at[m],
             device_id=(other, cross[j]), device_id_type=MESH,
         )
 
     def partial_copy(m, j):
         return pltpu.make_async_remote_copy(
             src_ref=psend.at[block(m, j)], dst_ref=pbuf.at[block(m, j)],
-            send_sem=p_send.at[m, j], recv_sem=p_recv.at[m, j],
+            send_sem=p_send.at[0], recv_sem=p_recv.at[m],
             device_id=(sec, peer[j]), device_id_type=MESH,
         )
 
-    def early_copy(m):
-        return pltpu.make_async_remote_copy(
-            src_ref=psend.at[block(m, PEERS - 1)], dst_ref=pbuf.at[block(m, PEERS - 1)],
-            send_sem=p_send.at[m, PEERS - 1], recv_sem=p_recv.at[m, PEERS - 1],
+    def piece(m, j, q):
+        return pl.ds((m * PEERS + j) * most + q * BF16_ROWS, BF16_ROWS)
+
+    def inward_copy(m, j, q):
+        return pltpu.make_async_remote_copy(
+            src_ref=psend.at[piece(m, j, q)], dst_ref=pbuf.at[piece(m, 5 - j, q)],
+            send_sem=p_send.at[0], recv_sem=p_recv.at[micros + (m * 2 + 3 - j) * pieces + q],
             device_id=(sec, peer[1]), device_id_type=MESH,
         )
+
+    def joined_copy(m, j, q):
+        return pltpu.make_async_remote_copy(
+            src_ref=psend.at[piece(m, j, q)], dst_ref=pbuf.at[piece(m, 0, q)],
+            send_sem=p_send.at[0], recv_sem=p_recv.at[m],
+            device_id=(sec, peer[j]), device_id_type=MESH,
+        )
+
+    def out_copy(m):
+        return pltpu.make_async_copy(base.at[m], out.at[m], l_sem.at[m])
 
     def pass_copy(src, dst, k):
         return pltpu.make_async_remote_copy(
@@ -192,13 +235,12 @@
             for j in range(PEERS - 2, 0, -1):
                 token_copy(m, j).start()
         for c in range(len(chunks)):
-            x_copy(c).start()
-            y_copy(c).start()
+            for copy in own_copies(c):
+                copy.start()
         pick_copy.start()
         pick_copy.wait_recv()
         gain_copy.wait_recv()
-        for m in range(micros):
-            token_copy(m, PEERS - 2).wait_send()
+        sent(x_send, 1, xbuf, micros * most)
         pl.semaphore_signal(go.at[0], inc=1, device_id=(other, me), device_id_type=MESH)
         for m in range(micros):
             early[share_of(m), :] = plain(turned(picked_in[m]), base[m])
@@ -209,8 +251,11 @@
                 token_relay(m).start()
         for c in range(len(chunks)):
             with jax.named_scope("wrelay"):
-                (y_copy if c % 2 == 0 else x_copy)(c).wait_recv()
+                (y_copy if c % 2 == 0 else x_copy)(c, True).wait_recv()
             turn_copy(c).start()
+        with jax.named_scope("xsent"):
+            sent(w_send, 2, weights.at[0], 3 * hid // 2)
+        pl.semaphore_signal(go.at[1], inc=1, device_id=(other, me), device_id_type=MESH)
 
     @pl.when(sec == 1)
     def _():
@@ -241,54 +286,52 @@
                 far_copy(c).wait_recv()
             far_turn_copy(c).start()
 
-    def wait_weights(some):
-        for c in some:
-            @pl.when(sec == 0)
-            def _():
-                (x_copy if c % 2 == 0 else y_copy)(c).wait_recv()
-                turn_copy(c).wait_recv()
-
-            @pl.when(sec == 1)
-            def _():
-                x_copy(c).wait_recv()
-                far_turn_copy(c).wait_recv()
+    def wait_weights(late, kinds):
+        @pl.when(sec == 0)
+        def _():
+            got(w_recv, count + late, weights.at[0], kinds * hid // 2)
+            got(w_recv, count + 2 + late, weights.at[0], kinds * hid // 2)
+            got(w_recv, count + 4 + late, weights.at[0], kinds * hid)
+
+        @pl.when(sec == 1)
+        def _():
+            got(w_recv, count + late, weights.at[0], kinds * hid)
+            got(w_recv, count + 4 + late, weights.at[0], kinds * hid)
 
     with jax.named_scope("ww"):
-        wait_weights(range(4))
+        wait_weights(0, 2)
 
     @pl.when(sec == 0)
     def _():
         with jax.named_scope("wtok"):
-            for m in range(micros):
-                token_copy(m, 1).wait_recv()
-                token_relay(m).wait_recv()
+            got(x_recv, micros, xbuf, 2 * micros * most)
 
     for m in range(micros):
         @pl.when(sec == 1)
         def _():
             with jax.named_scope("won"):
-                for j in range(PEERS):
-                    onward_copy(m, j).wait_recv()
+                got(x_recv, m, xbuf, PEERS * most)
 
         with jax.named_scope("gu"):
             x = xbuf[pl.ds(m * group_rows, group_rows), :]
             activated = (silu(across(x, weights[0])) * across(x, weights[1])).astype(jnp.bfloat16)
         if m == 0:
             with jax.named_scope("ww2"):
-                wait_weights(range(4, len(chunks)))
-
-            @pl.when(sec == 0)
-            def _():
-                pl.semaphore_signal(go.at[1], inc=1, device_id=(other, me), device_id_type=MESH)
-
+                wait_weights(1, 1)
         with jax.named_scope("down"):
             partial = plain(activated, weights[2])
             mine[share_of(m), :] = partial[0:most]
             psend[pl.ds(m * group_rows, group_rows), :] = partial.astype(jnp.bfloat16)
         @pl.when(sec == 0)
         def _():
-            across_part[share_of(m), :] = partial[2 * most:3 * most]
-            early_copy(m).start()
+            across_part[pl.ds(m * 2 * most, 2 * most), :] = partial[2 * most:4 * most]
+
+            @pl.when(outer)
+            def _():
+                for q in range(pieces):
+                    for j in (3, 2):
+                        inward_copy(m, j, q).start()
+
             if m == micros - 1:
                 for k in range(micros):
                     partial_copy(k, 1).start()
@@ -298,19 +341,17 @@
             for j in range(PEERS - 1, 0, -1):
                 partial_copy(m, j).start()
 
-    @pl.when(sec == 0)
-    def _():
-        for m in range(micros):
-            with jax.named_scope("wearly"):
-                early_copy(m).wait_recv()
-            joined = across_part[share_of(m), :] + pbuf[block(m, PEERS - 1), :].astype(jnp.float32)
-            psend[block(m, 2), :] = joined.astype(jnp.bfloat16)
-            partial_copy(m, 2).start()
-        for m in range(micros):
-            with jax.named_scope("wsent"):
-                partial_copy(m, 2).wait_send()
-        pl.semaphore_signal(go.at[2], inc=1, device_id=(other, me), device_id_type=MESH)
-
+    @pl.when((sec == 0) & inner)
+    def _():
+        for m in range(micros):
+            for q in range(pieces):
+                for j in (2, 3):
+                    with jax.named_scope("wearly"):
+                        inward_copy(m, 5 - j, q).wait_recv()
+                    mine_too = across_part[pl.ds((m * 2 + j - 2) * most + q * BF16_ROWS, BF16_ROWS), :]
+                    joined = mine_too + pbuf[piece(m, j, q), :].astype(jnp.float32)
+                    psend[piece(m, j, q), :] = joined.astype(jnp.bfloat16)
+                    joined_copy(m, j, q).start()
     @pl.when(sec == 1)
     def _():
         held_copy.wait_recv()
@@ -323,15 +364,27 @@
         with jax.named_scope("wpart"):
             score = jnp.sum(xbuf[block(m, 0), :].astype(jnp.float32) * router[...].astype(jnp.float32), axis=1, keepdims=True)
             share = 1.0 / (1.0 + jnp.exp(-score))
-            for j in range(1, PEERS - 1):
-                partial_copy(m, j).wait_recv()
-            last = partial_copy(m, PEERS - 1)
-            pl.when(sec == 1)(last.wait_recv)
-            update = mine[span, :]
-            for j in range(1, PEERS - 1):
-                update = update + pbuf[block(m, j), :].astype(jnp.float32)
-            over = pbuf[block(m, PEERS - 1), :].astype(jnp.float32)
-            update = update + jnp.where(sec == 1, over, 0.0)
+            @pl.when(sec == 0)
+            def _():
+                got(p_recv, m, pbuf, 2 * most)
+                if m == 0:
+                    pl.semaphore_signal(go.at[2], inc=1, device_id=(other, me), device_id_type=MESH)
+
+            @pl.when(sec == 1)
+            def _():
+                got(p_recv, m, pbuf, 3 * most)
+
+            update = mine[span, :] + pbuf[block(m, 1), :].astype(jnp.float32)
+
+            @pl.when(sec == 0)
+            def _():
+                rest[...] = pbuf[block(m, 0), :].astype(jnp.float32)
+
+            @pl.when(sec == 1)
+            def _():
+                rest[...] = pbuf[block(m, 2), :].astype(jnp.float32) + pbuf[block(m, 3), :].astype(jnp.float32)
+
+            update = update + rest[...]
         outc[span, :] = (held[span, :].astype(jnp.float32) + share * update).astype(jnp.bfloat16)
 
         @pl.when(sec == 0)
@@ -347,52 +400,35 @@
 
         @pl.when(sec == 1)
         def _():
-            out[m] = merge(m, picked, outc, base[m])
+            base[m] = merge(m, picked, outc, base[m])
+            out_copy(m).start()
 
     @pl.when(sec == 0)
     def _():
         held_copy.start()
         outc_copy.start()
         for m in range(micros):
-            out[m] = merge(m, picked, outc, base[m])
-
-    for c in range(len(chunks)):
-        x_copy(c).wait_send()
-
-        @pl.when(sec == 0)
-        def _():
-            y_copy(c).wait_send()
-            turn_copy(c).wait_send()
-
-        @pl.when(sec == 1)
-        def _():
-            far_copy(c).wait_send()
-            far_turn_copy(c).wait_send()
+            base[m] = merge(m, picked, outc, base[m])
+            out_copy(m).start()
+
+    sent(w_send, 0, weights.at[0], 3 * hid)
+    sent(w_send, 1, weights.at[0], 3 * hid)
     pick_copy.wait_send()
     for m in range(micros):
-        partial_copy(m, 1).wait_send()
-
-        @pl.when(sec == 0)
-        def _():
-            early_copy(m).wait_send()
-
-        @pl.when(sec == 1)
-        def _():
-            partial_copy(m, 2).wait_send()
-            partial_copy(m, PEERS - 1).wait_send()
+        out_copy(m).wait()
+    sent(p_send, 0, psend, 3 * micros * most)
 
     @pl.when(sec == 0)
     def _():
+        sent(w_send, 3, weights.at[0], 3 * hid // 2)
         held_copy.wait_send()
         outc_copy.wait_send()
-        for m in range(micros):
-            token_copy(m, 1).wait_send()
-            token_relay(m).wait_send()
-            for j in range(PEERS):
-                onward_copy(m, j).wait_send()
+        sent(x_send, 0, xbuf, 2 * micros * most)
+        sent(x_send, 2, xbuf, PEERS * micros * most)
 
     @pl.when(sec == 1)
     def _():
+        sent(w_send, 2, weights.at[0], 3 * hid)
         gain_copy.wait_send()
 
 
@@ -402,6 +438,8 @@
     most = rows // 4
     slots = n // PEERS
     own_rows = micros * most
+    chunks = 3 * (hid // BF16_ROWS)
+    pieces = most // BF16_ROWS
     all_rows = PEERS * own_rows
     dma = pltpu.SemaphoreType.DMA
     vmem = pl.BlockSpec(memory_space=pltpu.VMEM)
@@ -412,7 +450,7 @@
         functools.partial(kernel, n, most),
         out_shape=jax.ShapeDtypeStruct((micros, rows, width), jnp.bfloat16),
         in_specs=[whole, vmem, vmem, whole, whole, whole, vmem],
-        out_specs=vmem,
+        out_specs=whole,
         scratch_shapes=[
             half(micros, rows, width),
             half(own_rows, width),
@@ -429,9 +467,10 @@
             half(all_rows, width),
             half(all_rows, width),
             full(own_rows, width),
-            full(own_rows, width),
-            dma((slots, 6)), dma((slots, 6)),
-            dma((2 * micros, PEERS)), dma((micros, PEERS)), dma((micros, PEERS)), dma((micros, PEERS)),
+            full(2 * own_rows, width),
+            full(most, width),
+            dma((4,)), dma((chunks + 6,)),
+            dma((3,)), dma((micros + 1,)), dma((1,)), dma((micros + 2 * micros * pieces,)),
             dma((4,)), dma((4,)), dma((4,)),
             pltpu.SemaphoreType.REGULAR((3,)),
         ],
@@ -442,7 +481,33 @@
         tokens, norm_gains, router_cols.reshape(1, width),
         gate_weight[0, 0], up_weight[0, 0], down_weight[0, 0], jnp.swapaxes(expert_ids[0], 1, 2),
     )
-    return result[None]
+    return finish(result)[None]
+
+
+def finish_kernel(src, dst, hold, i_sem, o_sem):
+    micros, rows, width = src.shape
+    step = rows // CUTS
+    parts = [(m, pl.ds(c * step, step), m * CUTS + c) for m in range(micros) for c in range(CUTS)]
+    come = [pltpu.make_async_copy(src.at[m, r], hold.at[m, r], i_sem.at[k]) for m, r, k in parts]
+    leave = [pltpu.make_async_copy(hold.at[m, r], dst.at[m, r], o_sem.at[k]) for m, r, k in parts]
+    for copy in come:
+        copy.start()
+    for a, b in zip(come, leave):
+        a.wait()
+        b.start()
+    for copy in leave:
+        copy.wait()
+
+
+def finish(result):
+    whole = pl.BlockSpec(memory_space=pltpu.HBM)
+    return pl.pallas_call(
+        finish_kernel,
+        out_shape=jax.ShapeDtypeStruct(result.shape, result.dtype),
+        in_specs=[whole],
+        out_specs=whole,
+        scratch_shapes=[pltpu.VMEM(result.shape, result.dtype), pltpu.SemaphoreType.DMA((2 * CUTS,)), pltpu.SemaphoreType.DMA((2 * CUTS,))],
+    )(result)
 
 
 def gathered(tokens, norm_gains, router_cols, gate_weight, up_weight, down_weight, expert_ids):

time: 56.8 us -> 51.4 us (0.905)
  Pallas kernels: 54.2 us -> 51.2 us
  local copies, waits for them, and re-layouts: 2.3 us -> 0 us
    pallas_call x1, Pallas kernels: 54.2 us -> 49.2 us  [grouped(): pl.pallas_call(functools.partial(kernel, n, most), out_shape=jax.ShapeDty...]
    unnamed x1 -> x0, local copies, waits for them, and re-layouts: 2.3 us -> none
    pallas_call x0 -> x1, Pallas kernels: none -> 1.98 us  [finish(): pl.pallas_call(finish_kernel, out_shape=jax.ShapeDtypeStruct(result.shape...]
where the time goes in v2:
time: 51.4 us; the launch traced here: 51.2 us
  Pallas kernels  51.2 us (100%)
    pallas_call x1, Pallas kernels, grouped(): pl.pallas_call(functools.partial(kernel, n, most), out_shape=jax.ShapeDty...  49.2 us
    pallas_call x1, Pallas kernels, finish(): pl.pallas_call(finish_kernel, out_shape=jax.ShapeDtypeStruct(result.shape...  1.98 us

profile of v2, /device:TPU:1, one launch (start us, length us, event | category | flops | bytes accessed | tf_op | source)
XLA Modules:
  0.0 51.2 jit_solution(6702439884079497784)
XLA Ops:
  0.0 49.2 %shard_map.73.src = bf16[2,128,2048]{2,1,0:T(8,128)(2,1)} custom-call(bf16[2,128,2048]{2,1,0:T(8,128)(2,1)} %tokens.1, f32[1,2048]{1,0:T(1,128)} %gain.1, bf16[1,2048]{1,0:T(2,128)(2,1)} %bitcast.11, bf16[64,2048]{1,0:T(8,128)(2,1)} %bitcast.8, bf16[64,2048]{1,0:T(8,128)(2,1)} %bitcast.9, bf16[64,2048]{1,0:T(8,128)(2,1)} %bitcast.10, s32[2,8,128]{2,1,0:T(8,128)} %bitcast.12), custom_call_target="tpu_custom_call" | custom-call | tf_op jit(solution)/shard_map/pallas_call | solution.py:449
  49.2 2.0 %shard_map.74 = bf16[2,128,2048]{2,1,0:T(8,128)(2,1)} custom-call(bf16[2,128,2048]{2,1,0:T(8,128)(2,1)} %shard_map.73.src), custom_call_target="tpu_custom_call" | custom-call | tf_op jit(solution)/shard_map/pallas_call | solution.py:504

commit v3 on v2

--- a/solution.py
+++ b/solution.py
@@ -11,6 +11,7 @@
 BF16_ROWS = 16
 PEERS = 4
 AHEAD = 10
+LEFT = 4
 CUTS = 2
 FIRST = 0
 EPS = 1e-05
@@ -30,9 +31,9 @@
 
 def kernel(
     n, most,
-    tokens, gain, router, gate, up, down, ids,
+    tokens, gain_at, router_at, gate, up, down, ids_at,
     out,
-    base, held, hnext, early, weights, picked, picked_in, gain_in, outc, outc_in, xbuf, xnext, pbuf, psend, mine, across_part, rest,
+    gain, router, ids, base, held, hnext, early, weights, picked, picked_in, gain_in, outc, outc_in, xbuf, xnext, pbuf, psend, mine, across_part, rest,
     w_send, w_recv, x_send, x_recv, p_send, p_recv, o_send, o_recv, l_sem, go,
 ):
     sec = lax.axis_index("section")
@@ -66,9 +67,10 @@
     own = (gate, up, down)
     chunks = [(a, h) for a in range(3) for h in range(parts)]
 
+    small = [pltpu.make_async_copy(src, dst, l_sem.at[4 + k]) for k, (src, dst) in enumerate([(ids_at, ids), (gain_at, gain), (router_at, router)])]
     fetch = [pltpu.make_async_copy(tokens, base, l_sem.at[3])]
     fetch += [pltpu.make_async_copy(own[a], weights.at[a, pl.ds(0, hid)], l_sem.at[a]) for a in range(3)]
-    for copy in fetch:
+    for copy in small + fetch[:1]:
         copy.start()
 
     def weight_copy(slot, chunk, target, send, recv, source_slot=None):
@@ -107,7 +109,7 @@
 
     def turn_copy(chunk):
         if chunk % 2 == 0:
-            return weight_copy(3, chunk, at_x, 2, group(2, chunk), 2)
+            return weight_copy(3, chunk, at_x, 2 if chunk < 2 * LEFT else 4, group(2, chunk), 2)
         return weight_copy(3, chunk, at_y, 3, group(2, chunk), 1)
 
     def far_turn_copy(chunk):
@@ -149,9 +151,9 @@
             device_id=(sec, peer[1]), device_id_type=MESH,
         )
 
-    def onward_copy(m, j):
-        return pltpu.make_async_remote_copy(
-            src_ref=xnext.at[share_of(m)], dst_ref=xbuf.at[block(m, j)],
+    def onward_copy(m, j, q):
+        return pltpu.make_async_remote_copy(
+            src_ref=xnext.at[pl.ds(m * most + q * BF16_ROWS, BF16_ROWS)], dst_ref=xbuf.at[piece(m, j, q)],
             send_sem=x_send.at[2], recv_sem=x_recv.at[m],
             device_id=(other, cross[j]), device_id_type=MESH,
         )
@@ -171,6 +173,13 @@
             src_ref=psend.at[piece(m, j, q)], dst_ref=pbuf.at[piece(m, 5 - j, q)],
             send_sem=p_send.at[0], recv_sem=p_recv.at[micros + (m * 2 + 3 - j) * pieces + q],
             device_id=(sec, peer[1]), device_id_type=MESH,
+        )
+
+    def share_copy(m, j, q):
+        return pltpu.make_async_remote_copy(
+            src_ref=psend.at[piece(m, j, q)], dst_ref=pbuf.at[piece(m, j, q)],
+            send_sem=p_send.at[0], recv_sem=p_recv.at[m],
+            device_id=(sec, peer[j]), device_id_type=MESH,
         )
 
     def joined_copy(m, j, q):
@@ -207,6 +216,8 @@
         return jnp.where(chosen, placed, under.astype(jnp.float32)).astype(jnp.bfloat16)
 
     with jax.named_scope("pick"):
+        for copy in small:
+            copy.wait()
         at_row = lax.broadcasted_iota(jnp.int32, (rows, rows), 0)
         at_col = lax.broadcasted_iota(jnp.int32, (rows, rows), 1)
         lower = jnp.where(at_row >= at_col, 1.0, 0.0).astype(jnp.bfloat16)
@@ -216,8 +227,9 @@
             rank = plain(lower, spread.astype(jnp.bfloat16))
             hit = (rank.astype(jnp.int32) - 1 == at_col) & (spread > 0.5)
             picked[m] = jnp.where(hit, 1.0, 0.0).astype(jnp.bfloat16)
-        for copy in fetch:
-            copy.wait()
+        fetch[0].wait()
+    for copy in fetch[1:]:
+        copy.start()
 
     @pl.when(sec == 0)
     def _():
@@ -254,7 +266,7 @@
                 (y_copy if c % 2 == 0 else x_copy)(c, True).wait_recv()
             turn_copy(c).start()
         with jax.named_scope("xsent"):
-            sent(w_send, 2, weights.at[0], 3 * hid // 2)
+            sent(w_send, 2, weights.at[0], LEFT * half)
         pl.semaphore_signal(go.at[1], inc=1, device_id=(other, me), device_id_type=MESH)
 
     @pl.when(sec == 1)
@@ -298,6 +310,8 @@
             got(w_recv, count + late, weights.at[0], kinds * hid)
             got(w_recv, count + 4 + late, weights.at[0], kinds * hid)
 
+    for copy in fetch[1:]:
+        copy.wait()
     with jax.named_scope("ww"):
         wait_weights(0, 2)
 
@@ -339,7 +353,8 @@
         @pl.when(sec == 1)
         def _():
             for j in range(PEERS - 1, 0, -1):
-                partial_copy(m, j).start()
+                for q in range(pieces):
+                    share_copy(m, j, q).start()
 
     @pl.when((sec == 0) & inner)
     def _():
@@ -396,7 +411,8 @@
                 xnext[span, :] = norm(following, gain_in[...])
                 hnext[span, :] = following.astype(jnp.bfloat16)
             for j in range(PEERS - 1, -1, -1):
-                onward_copy(m, j).start()
+                for q in range(pieces):
+                    onward_copy(m, j, q).start()
 
         @pl.when(sec == 1)
         def _():
@@ -421,6 +437,7 @@
     @pl.when(sec == 0)
     def _():
         sent(w_send, 3, weights.at[0], 3 * hid // 2)
+        sent(w_send, 4, weights.at[0], (count // 2 - LEFT) * half)
         held_copy.wait_send()
         outc_copy.wait_send()
         sent(x_send, 0, xbuf, 2 * micros * most)
@@ -442,16 +459,18 @@
     pieces = most // BF16_ROWS
     all_rows = PEERS * own_rows
     dma = pltpu.SemaphoreType.DMA
-    vmem = pl.BlockSpec(memory_space=pltpu.VMEM)
     whole = pl.BlockSpec(memory_space=pltpu.HBM)
     half = lambda *shape: pltpu.VMEM(shape, jnp.bfloat16)
     full = lambda *shape: pltpu.VMEM(shape, jnp.float32)
     result = pl.pallas_call(
         functools.partial(kernel, n, most),
         out_shape=jax.ShapeDtypeStruct((micros, rows, width), jnp.bfloat16),
-        in_specs=[whole, vmem, vmem, whole, whole, whole, vmem],
+        in_specs=[whole] * 7,
         out_specs=whole,
         scratch_shapes=[
+            full(1, width),
+            half(1, width),
+            pltpu.VMEM(expert_ids.shape[1:2] + expert_ids.shape[3:1:-1], jnp.int32),
             half(micros, rows, width),
             half(own_rows, width),
             half(own_rows, width),
@@ -469,9 +488,9 @@
             full(own_rows, width),
             full(2 * own_rows, width),
             full(most, width),
-            dma((4,)), dma((chunks + 6,)),
+            dma((5,)), dma((chunks + 6,)),
             dma((3,)), dma((micros + 1,)), dma((1,)), dma((micros + 2 * micros * pieces,)),
-            dma((4,)), dma((4,)), dma((4,)),
+            dma((4,)), dma((4,)), dma((7,)),
             pltpu.SemaphoreType.REGULAR((3,)),
         ],
         compiler_params=pltpu.CompilerParams(

time: 51.4 us -> 50.4 us (0.981)
  Pallas kernels: 51.2 us -> 50.2 us
    pallas_call x1, Pallas kernels: 49.2 us -> 48.3 us  [grouped(): pl.pallas_call(functools.partial(kernel, n, most), out_shape=jax.ShapeDty...]
where the time goes in v3:
time: 50.4 us; the launch traced here: 50.2 us
  Pallas kernels  50.2 us (100%)
    pallas_call x1, Pallas kernels, grouped(): pl.pallas_call(functools.partial(kernel, n, most), out_shape=jax.ShapeDty...  48.3 us
    pallas_call x1, Pallas kernels, finish(): pl.pallas_call(finish_kernel, out_shape=jax.ShapeDtypeStruct(result.shape...  1.98 us

profile of v3, /device:TPU:1, one launch (start us, length us, event | category | flops | bytes accessed | tf_op | source)
XLA Modules:
  0.0 50.2 jit_solution(135489561113477999)
XLA Ops:
  0.0 48.3 %shard_map.73.src = bf16[2,128,2048]{2,1,0:T(8,128)(2,1)} custom-call(bf16[2,128,2048]{2,1,0:T(8,128)(2,1)} %tokens.1, f32[1,2048]{1,0:T(1,128)} %gain_at.1, bf16[1,2048]{1,0:T(2,128)(2,1)} %bitcast.11, bf16[64,2048]{1,0:T(8,128)(2,1)} %bitcast.8, bf16[64,2048]{1,0:T(8,128)(2,1)} %bitcast.9, bf16[64,2048]{1,0:T(8,128)(2,1)} %bitcast.10, s32[2,8,128]{2,1,0:T(8,128)} %bitcast.12), custom_call_target="tpu_custom_call" | custom-call | tf_op jit(solution)/shard_map/pallas_call | solution.py:465
  48.3 2.0 %shard_map.74 = bf16[2,128,2048]{2,1,0:T(8,128)(2,1)} custom-call(bf16[2,128,2048]{2,1,0:T(8,128)(2,1)} %shard_map.73.src), custom_call_target="tpu_custom_call" | custom-call | tf_op jit(solution)/shard_map/pallas_call | solution.py:523

commit v4 on v3

--- a/solution.py
+++ b/solution.py
@@ -12,7 +12,6 @@
 PEERS = 4
 AHEAD = 10
 LEFT = 4
-CUTS = 2
 FIRST = 0
 EPS = 1e-05
 
@@ -466,7 +465,7 @@
         functools.partial(kernel, n, most),
         out_shape=jax.ShapeDtypeStruct((micros, rows, width), jnp.bfloat16),
         in_specs=[whole] * 7,
-        out_specs=whole,
+        out_specs=pl.BlockSpec(memory_space=pl.ANY),
         scratch_shapes=[
             full(1, width),
             half(1, width),
@@ -494,38 +493,33 @@
             pltpu.SemaphoreType.REGULAR((3,)),
         ],
         compiler_params=pltpu.CompilerParams(
-            collective_id=0, has_side_effects=True, vmem_limit_bytes=67_000_000
+            collective_id=0, has_side_effects=True, vmem_limit_bytes=24_000_000
         ),
     )(
-        tokens, norm_gains, router_cols.reshape(1, width),
-        gate_weight[0, 0], up_weight[0, 0], down_weight[0, 0], jnp.swapaxes(expert_ids[0], 1, 2),
+        *[pltpu.with_memory_space_constraint(a, pltpu.HBM) for a in (
+            tokens, norm_gains, router_cols.reshape(1, width),
+            gate_weight[0, 0], up_weight[0, 0], down_weight[0, 0], jnp.swapaxes(expert_ids[0], 1, 2),
+        )]
     )
     return finish(result)[None]
 
 
-def finish_kernel(src, dst, hold, i_sem, o_sem):
-    micros, rows, width = src.shape
-    step = rows // CUTS
-    parts = [(m, pl.ds(c * step, step), m * CUTS + c) for m in range(micros) for c in range(CUTS)]
-    come = [pltpu.make_async_copy(src.at[m, r], hold.at[m, r], i_sem.at[k]) for m, r, k in parts]
-    leave = [pltpu.make_async_copy(hold.at[m, r], dst.at[m, r], o_sem.at[k]) for m, r, k in parts]
-    for copy in come:
+def finish_kernel(src, dst, sem):
+    copies = [pltpu.make_async_copy(src.at[m], dst.at[m], sem.at[m]) for m in range(src.shape[0])]
+    for copy in copies:
         copy.start()
-    for a, b in zip(come, leave):
-        a.wait()
-        b.start()
-    for copy in leave:
+    for copy in copies:
         copy.wait()
 
 
 def finish(result):
-    whole = pl.BlockSpec(memory_space=pltpu.HBM)
     return pl.pallas_call(
         finish_kernel,
         out_shape=jax.ShapeDtypeStruct(result.shape, result.dtype),
-        in_specs=[whole],
-        out_specs=whole,
-        scratch_shapes=[pltpu.VMEM(result.shape, result.dtype), pltpu.SemaphoreType.DMA((2 * CUTS,)), pltpu.SemaphoreType.DMA((2 * CUTS,))],
+        in_specs=[pl.BlockSpec(memory_space=pl.ANY)],
+        out_specs=pl.BlockSpec(memory_space=pltpu.HBM),
+        scratch_shapes=[pltpu.SemaphoreType.DMA((result.shape[0],))],
+        compiler_params=pltpu.CompilerParams(vmem_limit_bytes=4_000_000),
     )(result)
 
 

time: 50.4 us -> 48.7 us (0.966)
  Pallas kernels: 50.2 us -> 48.5 us
    pallas_call x1, Pallas kernels: 1.98 us -> 0.99 us  [finish(): pl.pallas_call(finish_kernel, out_shape=jax.ShapeDtypeStruct(result.shape...]
    pallas_call x1, Pallas kernels: 48.3 us -> 47.5 us  [grouped(): pl.pallas_call(functools.partial(kernel, n, most), out_shape=jax.ShapeDty...]
where the time goes in v4:
time: 48.7 us; the launch traced here: 48.5 us
  Pallas kernels  48.5 us (100%)
    pallas_call x1, Pallas kernels, grouped(): pl.pallas_call(functools.partial(kernel, n, most), out_shape=jax.ShapeDty...  47.5 us
    pallas_call x1, Pallas kernels, finish(): pl.pallas_call(finish_kernel, out_shape=jax.ShapeDtypeStruct(result.shape...  0.99 us

profile of v4, /device:TPU:1, one launch (start us, length us, event | category | flops | bytes accessed | tf_op | source)
XLA Modules:
  0.0 48.5 jit_solution(10413028135166021821)
XLA Ops:
  0.0 47.5 %shard_map.73.src = bf16[2,128,2048]{2,1,0:T(8,128)(2,1)S(1)} custom-call(bf16[2,128,2048]{2,1,0:T(8,128)(2,1)} %tokens.1, f32[1,2048]{1,0:T(1,128)} %gain_at.1, bf16[1,2048]{1,0:T(2,128)(2,1)} %bitcast.11, bf16[64,2048]{1,0:T(8,128)(2,1)} %bitcast.8, bf16[64,2048]{1,0:T(8,128)(2,1)} %bitcast.9, bf16[64,2048]{1,0:T(8,128)(2,1)} %bitcast.10, ...), custom_call_target="tpu_custom_call" | custom-call | tf_op jit(solution)/shard_map/pallas_call | solution.py:464
  47.5 1.0 %shard_map.74 = bf16[2,128,2048]{2,1,0:T(8,128)(2,1)} custom-call(bf16[2,128,2048]{2,1,0:T(8,128)(2,1)S(1)} %shard_map.73.src), custom_call_target="tpu_custom_call" | custom-call | tf_op jit(solution)/shard_map/pallas_call | solution.py:516
